TPU v7x, 128 devices: a whole 4x4x4 slice. The times are simulated.
128 devices in a mesh: corpus: 32 (over y, z, core), query: 4 (over x).
Axes of the slice: x: 4, y: 4, z: 4, core: 2. Of those that a mesh axis runs over, the one named last changes fastest.
Arguments:
- queries: bfloat16 [32768, 768], P(('corpus', 'query')), may hold values from -8 to 8
- probes: int32 [32768, 4], P(('corpus', 'query')), may hold values from 0 to 1023, as said below
- targets: int32 [32768, 8], P(('corpus', 'query')), may hold values from 0 to 4095, all different within a row
- passage_codes: int32 [1024, 96, 1024], P('corpus'), may hold values from 0 to 15
- codebook: float32 [16, 768], replicated, may hold values from -6 to 6
Outputs:
- grad_queries: bfloat16 [32768, 768], P(('corpus', 'query'))
- codebook_step: float32 [16, 768], replicated
Inputs may be any that keep to these rules, and one draw needn't show every extreme that they name: `probes`: each row names 4 different lists; list l belongs to index l // 32 of corpus. In every aligned block of 256 rows (the rows of one device) no list is named more than 2 times, and one list, the same one in every block, is named exactly 2 times. `targets`: each row names 8 different candidates; column r holds the candidate of rank r.
All inputs are finite; a program needn't handle non-finite values.
Results may differ from a plain program's by a relative error of at most 0.01.
The roundings to bfloat16 on the way count: a program that leaves them out, or rounds other values in their place, can miss the bound.
Values may be sent and summed in bfloat16 or wider, within the bound.
No kernel may reach another device: no remote copies, remote signals or barrier semaphores. Data moves between devices by JAX's collectives and lax.ppermute only.
A program may use at most 192 MiB of HBM per device.

v0:
```python
import jax
import jax.numpy as jnp
from jax import lax
from jax.sharding import PartitionSpec as P

D = 768
SUBSPACES = 96
CENTROIDS = 16
SUBDIM = 8
PASSAGES = 1024
PROBES = 4
TARGETS = 8
NEGATIVE = -1e30
EPSILON = 1e-06


def rank_weights():
    levels = jnp.arange(TARGETS, dtype=jnp.int32).astype(jnp.float32)
    return 2.0 * (TARGETS - levels) / (TARGETS * (TARGETS + 1.0))


def rank_slots(list_keys, key_count, keep):
    key_ids = jnp.arange(key_count, dtype=jnp.int32)
    marked = ((list_keys[:, None] == key_ids[None, :]) & keep[:, None]).astype(jnp.int32)
    running = jnp.cumsum(marked, axis=0)
    return jnp.sum(marked * running, axis=1) - 1


def note_block(probes, targets):
    row_count = probes.shape[0]
    probe_cols = jnp.arange(PROBES, dtype=jnp.int32)
    inside = targets[:, None, :] // PASSAGES == probe_cols[None, :, None]
    target_spot = jnp.where(inside, targets[:, None, :] % PASSAGES, -1)
    query_ids = jnp.broadcast_to(
        jnp.arange(row_count, dtype=jnp.int32)[:, None, None], (row_count, PROBES, 1)
    )
    return jnp.concatenate([query_ids, target_spot], axis=2).reshape(
        row_count * PROBES, TARGETS + 1
    )


def lookup_rows(rows_block, codebook):
    lead_shape = rows_block.shape[:-1]
    split_rows = rows_block.astype(jnp.float32).reshape(lead_shape + (SUBSPACES, SUBDIM))
    centroids = codebook.reshape(CENTROIDS, SUBSPACES, SUBDIM)
    lut_rows = jnp.einsum(
        "...me,kme->...mk", split_rows, centroids, precision=lax.Precision.HIGHEST
    )
    return lut_rows.reshape(lead_shape + (SUBSPACES * CENTROIDS,)).astype(jnp.bfloat16)


def code_one_hot(code_block):
    levels = jnp.arange(CENTROIDS, dtype=jnp.int32)
    marked = code_block[:, :, None, :] == levels[None, None, :, None]
    return marked.astype(jnp.bfloat16).reshape(
        code_block.shape[0], SUBSPACES * CENTROIDS, code_block.shape[2]
    )


def group_size(lists_dev, slot_rows):
    group_width = 1
    while (
        group_width * 2 <= lists_dev
        and lists_dev % (group_width * 2) == 0
        and (group_width * slot_rows < 512)
    ):
        group_width = group_width * 2
    return group_width


def first_pass(got_rows, passage_codes, codebook, group_width):
    lists_dev, slot_rows = (got_rows.shape[0], got_rows.shape[1])
    groups = lists_dev // group_width

    def score_piece(pieces):
        row_group, code_group = pieces
        lut_rows = lookup_rows(row_group, codebook)
        one_hot = code_one_hot(code_group)
        scores = jnp.einsum("grk,gkl->grl", lut_rows, one_hot, preferred_element_type=jnp.float32)
        top_score = jnp.max(scores, axis=2)
        exp_total = jnp.sum(jnp.exp(scores - top_score[:, :, None]), axis=2)
        return (scores, top_score, exp_total)

    scores, top_score, exp_total = lax.map(
        score_piece,
        (
            got_rows.reshape(groups, group_width, slot_rows, D),
            passage_codes.reshape(groups, group_width, SUBSPACES, PASSAGES),
        ),
    )
    return (
        scores.reshape(lists_dev, slot_rows, PASSAGES),
        top_score.reshape(lists_dev, slot_rows),
        exp_total.reshape(lists_dev, slot_rows),
    )


def second_pass(
    got_rows, got_notes, passage_codes, codebook, scores, query_top, query_total, group_width
):
    lists_dev, slot_rows = (got_rows.shape[0], got_rows.shape[1])
    groups = lists_dev // group_width
    weights = rank_weights()
    places = jnp.arange(PASSAGES, dtype=jnp.int32)
    centroids = codebook.reshape(CENTROIDS, SUBSPACES, SUBDIM)
    highest = lax.Precision.HIGHEST

    def grad_piece(pieces):
        row_group, note_group, code_group, score_group, top_group, total_group = pieces
        one_hot = code_one_hot(code_group)
        target_spot = note_group[:, :, 1:]
        teacher = jnp.sum(
            jnp.where(target_spot[:, :, :, None] == places, weights[:, None], 0.0), axis=2
        )
        student = jnp.exp(score_group - top_group[:, :, None]) / total_group[:, :, None]
        is_valid = note_group[:, :, 0] >= 0
        grad_scores = jnp.where(is_valid[:, :, None], student - teacher, 0.0).astype(jnp.bfloat16)
        histogram = jnp.einsum(
            "grl,gkl->grk", grad_scores, one_hot, preferred_element_type=jnp.float32
        )
        histogram = histogram.reshape(group_width, slot_rows, SUBSPACES, CENTROIDS)
        partial_value = jnp.einsum("grmk,kme->grme", histogram, centroids, precision=highest)
        split_rows = row_group.astype(jnp.float32).reshape(
            group_width, slot_rows, SUBSPACES, SUBDIM
        )
        book_part = jnp.einsum("grmk,grme->kme", histogram, split_rows, precision=highest)
        return (partial_value.reshape(group_width, slot_rows, D), book_part)

    partial_value, book_part = lax.map(
        grad_piece,
        (
            got_rows.reshape(groups, group_width, slot_rows, D),
            got_notes.reshape(groups, group_width, slot_rows, TARGETS + 1),
            passage_codes.reshape(groups, group_width, SUBSPACES, PASSAGES),
            scores.reshape(groups, group_width, slot_rows, PASSAGES),
            query_top.reshape(groups, group_width, slot_rows),
            query_total.reshape(groups, group_width, slot_rows),
        ),
    )
    return (
        partial_value.reshape(lists_dev, slot_rows, D),
        jnp.sum(book_part, axis=0).reshape(CENTROIDS, D),
    )


def shards(queries, probes, targets, passage_codes, codebook):
    corpus_size = lax.axis_size("corpus")
    query_rows = queries.shape[0]
    lists_dev = passage_codes.shape[0]
    list_total = lists_dev * corpus_size
    capacity = min(query_rows, max(2, 2 * PROBES * query_rows // list_total))
    slot_rows = corpus_size * capacity
    slot_count = lists_dev * slot_rows
    group_width = group_size(lists_dev, slot_rows)
    flat_probes = probes.reshape(-1)
    local_list = flat_probes % lists_dev
    owner_ids = flat_probes // lists_dev
    slot_rank = rank_slots(flat_probes, list_total, jnp.ones(flat_probes.shape, jnp.bool_))
    note_rows = note_block(probes, targets)
    placed = (local_list * corpus_size + owner_ids) * capacity + slot_rank
    sending = (
        jnp.zeros((slot_count, D), jnp.bfloat16).at[placed].set(jnp.repeat(queries, PROBES, axis=0))
    )
    note_buffer = jnp.full((slot_count, TARGETS + 1), -1, jnp.int32).at[placed].set(note_rows)
    got_rows, got_notes = (
        lax.all_to_all(
            sending.reshape(lists_dev, corpus_size, capacity, D),
            "corpus",
            split_axis=1,
            concat_axis=1,
            tiled=True,
        ),
        lax.all_to_all(
            note_buffer.reshape(lists_dev, corpus_size, capacity, TARGETS + 1),
            "corpus",
            split_axis=1,
            concat_axis=1,
            tiled=True,
        ),
    )
    got_rows = got_rows.reshape(lists_dev, slot_rows, D)
    got_notes = got_notes.reshape(lists_dev, slot_rows, TARGETS + 1)
    is_valid = got_notes[:, :, 0] >= 0
    scores, top_score, exp_total = first_pass(got_rows, passage_codes, codebook, group_width)
    top_score = jnp.where(is_valid, top_score, NEGATIVE)
    exp_total = jnp.where(is_valid, exp_total, 0.0)
    back_top, back_total = (
        lax.all_to_all(
            top_score.reshape(lists_dev, corpus_size, capacity),
            "corpus",
            split_axis=1,
            concat_axis=1,
            tiled=True,
        ),
        lax.all_to_all(
            exp_total.reshape(lists_dev, corpus_size, capacity),
            "corpus",
            split_axis=1,
            concat_axis=1,
            tiled=True,
        ),
    )
    entry_top = back_top.reshape(-1)[placed].reshape(query_rows, PROBES)
    entry_total = back_total.reshape(-1)[placed].reshape(query_rows, PROBES)
    own_top = jnp.max(entry_top, axis=1)
    own_total = jnp.sum(entry_total * jnp.exp(entry_top - own_top[:, None]), axis=1)
    slot_top = jnp.zeros((slot_count,), jnp.float32).at[placed].set(jnp.repeat(own_top, PROBES))
    slot_total = jnp.ones((slot_count,), jnp.float32).at[placed].set(jnp.repeat(own_total, PROBES))
    query_top, query_total = (
        lax.all_to_all(
            slot_top.reshape(lists_dev, corpus_size, capacity),
            "corpus",
            split_axis=1,
            concat_axis=1,
            tiled=True,
        ),
        lax.all_to_all(
            slot_total.reshape(lists_dev, corpus_size, capacity),
            "corpus",
            split_axis=1,
            concat_axis=1,
            tiled=True,
        ),
    )
    query_top = query_top.reshape(lists_dev, slot_rows)
    query_total = query_total.reshape(lists_dev, slot_rows)
    query_top = jnp.where(is_valid, query_top, 0.0)
    query_total = jnp.where(is_valid, query_total, 1.0)
    partial_value, book_part = second_pass(
        got_rows, got_notes, passage_codes, codebook, scores, query_top, query_total, group_width
    )
    returned = lax.all_to_all(
        partial_value.reshape(lists_dev, corpus_size, capacity, D),
        "corpus",
        split_axis=1,
        concat_axis=1,
        tiled=True,
    )
    per_probe = returned.reshape(slot_count, D)[placed].reshape(query_rows, PROBES, D)
    grad_queries = jnp.sum(per_probe, axis=1)
    book_sum = lax.psum(book_part, ("corpus", "query"))
    normed = book_sum * lax.rsqrt(jnp.mean(book_sum * book_sum) + EPSILON)
    return (grad_queries.astype(jnp.bfloat16), normed)


def solution(mesh):
    placed = (
        P(("corpus", "query"), None),
        P(("corpus", "query"), None),
        P(("corpus", "query"), None),
        P("corpus", None, None),
        P(),
    )
    return jax.shard_map(
        shards,
        mesh=mesh,
        in_specs=placed,
        out_specs=(P(("corpus", "query"), None), P()),
        check_vma=False,
    )
```

profile of v0, /device:TPU:1, one launch (start us, length us, event | category | flops | bytes accessed | tf_op | source)
XLA Modules:
  0.0 697.2 jit_solution(16750538512104853884)
XLA Ops:
  16.7 9.6 %all-to-all-start = ((s32[32,1,576]{2,1,0:T(1,128)}), s32[32,1,576]{2,1,0:T(1,128)S(1)}, u32[]{:S(2)}, u32[]{:S(2)}) async-start(s32[32,1,576]{2,1,0:T(1,128)} %reshape.393), calls=%async_computation | async-start | bytes 163840 | tf_op jit(solution)/shard_map/all_to_all | solution.py:173
  60.2 31.6 %all-to-all-done.1 = bf16[32,32,2,768]{3,2,0,1:T(2,128)(2,1)S(1)} async-done(((bf16[32,32,2,768]{3,2,0,1:T(2,128)(2,1)}), bf16[32,32,2,768]{3,2,0,1:T(2,128)(2,1)S(1)}, u32[]{:S(2)}, u32[]{:S(2)}) %all-to-all-start.1) | async-done | bytes 3145760 | tf_op jit(solution)/shard_map/all_to_all | solution.py:166
  102.7 129.6 %while.27 = (s32[]{:T(128)}, f32[4,8,64,1024]{3,2,1,0:T(8,128)}, f32[4,8,64]{2,1,0:T(8,128)}, f32[4,8,64]{2,1,0:T(8,128)}, bf16[4,8,64,768]{2,3,1,0:T(8,128)(2,1...) while((s32[]{:T(128)}, f32[4,8,64,1024]{3,2,1,0:T(8,128)}, ...), condition=%wide.region_8.9_spmd, body=%wide.region_5.8_spmd.sunk | while | flops 1701051392 | bytes 57241216 | solution.py:84
  112.8 9.4 %bitcast_compare_fusion.4 = pred[8,1536,1024]{2,1,0:T(32,128)(4,1)} fusion(s32[1536]{0:T(1024)S(1)} %eq.177, s32[8,96,1024]{2,1,0:T(8,128)S(1)} %dynamic-slice_bitcast_fusion.14), kind=kLoop, calls=%fused_computation.9.clone.1 | loop fusion | flops 12582912 | bytes 15734784 | tf_op jit(solution)/shard_map/while/body/eval_jaxpr/eq | solution.py:54
  122.1 11.7 %bitcast_dynamic-update-slice_fusion.5 = (f32[4,8,64,1024]{3,2,1,0:T(8,128)}, f32[8,64,1024]{2,1,0:T(8,128)S(1)}) fusion(f32[4,8,64,1024]{3,2,1,0:T(8,128)} %get-tuple-element.387, s32[]{:T(128)} %get-tuple-element.386, bf16[8,64,1536]{1,2,0:T(8,128)(2,1)S(1)} %bitcast.165, pred[8,1536,1024]{2,1,0:T(32,128)(4,1)} %bitcast_compare_fusion.4), kind=kOutput, calls=%fused_computation.12.clone.1 | convolution fusion | flops 1610612736 | bytes 18350592 | tf_op jit(solution)/shard_map/while/body/eval_jaxpr/grk,gkl->grl/dot_general | solution.py:79
  145.2 9.4 %bitcast_compare_fusion.4 = pred[8,1536,1024]{2,1,0:T(32,128)(4,1)} fusion(s32[1536]{0:T(1024)S(1)} %eq.177, s32[8,96,1024]{2,1,0:T(8,128)S(1)} %dynamic-slice_bitcast_fusion.14), kind=kLoop, calls=%fused_computation.9.clone.1 | loop fusion | flops 12582912 | bytes 15734784 | tf_op jit(solution)/shard_map/while/body/eval_jaxpr/eq | solution.py:54
  154.5 11.7 %bitcast_dynamic-update-slice_fusion.5 = (f32[4,8,64,1024]{3,2,1,0:T(8,128)}, f32[8,64,1024]{2,1,0:T(8,128)S(1)}) fusion(f32[4,8,64,1024]{3,2,1,0:T(8,128)} %get-tuple-element.387, s32[]{:T(128)} %get-tuple-element.386, bf16[8,64,1536]{1,2,0:T(8,128)(2,1)S(1)} %bitcast.165, pred[8,1536,1024]{2,1,0:T(32,128)(4,1)} %bitcast_compare_fusion.4), kind=kOutput, calls=%fused_computation.12.clone.1 | convolution fusion | flops 1610612736 | bytes 18350592 | tf_op jit(solution)/shard_map/while/body/eval_jaxpr/grk,gkl->grl/dot_general | solution.py:79
  177.6 9.4 %bitcast_compare_fusion.4 = pred[8,1536,1024]{2,1,0:T(32,128)(4,1)} fusion(s32[1536]{0:T(1024)S(1)} %eq.177, s32[8,96,1024]{2,1,0:T(8,128)S(1)} %dynamic-slice_bitcast_fusion.14), kind=kLoop, calls=%fused_computation.9.clone.1 | loop fusion | flops 12582912 | bytes 15734784 | tf_op jit(solution)/shard_map/while/body/eval_jaxpr/eq | solution.py:54
  186.9 11.7 %bitcast_dynamic-update-slice_fusion.5 = (f32[4,8,64,1024]{3,2,1,0:T(8,128)}, f32[8,64,1024]{2,1,0:T(8,128)S(1)}) fusion(f32[4,8,64,1024]{3,2,1,0:T(8,128)} %get-tuple-element.387, s32[]{:T(128)} %get-tuple-element.386, bf16[8,64,1536]{1,2,0:T(8,128)(2,1)S(1)} %bitcast.165, pred[8,1536,1024]{2,1,0:T(32,128)(4,1)} %bitcast_compare_fusion.4), kind=kOutput, calls=%fused_computation.12.clone.1 | convolution fusion | flops 1610612736 | bytes 18350592 | tf_op jit(solution)/shard_map/while/body/eval_jaxpr/grk,gkl->grl/dot_general | solution.py:79
  210.0 9.4 %bitcast_compare_fusion.4 = pred[8,1536,1024]{2,1,0:T(32,128)(4,1)} fusion(s32[1536]{0:T(1024)S(1)} %eq.177, s32[8,96,1024]{2,1,0:T(8,128)S(1)} %dynamic-slice_bitcast_fusion.14), kind=kLoop, calls=%fused_computation.9.clone.1 | loop fusion | flops 12582912 | bytes 15734784 | tf_op jit(solution)/shard_map/while/body/eval_jaxpr/eq | solution.py:54
  219.4 11.7 %bitcast_dynamic-update-slice_fusion.5 = (f32[4,8,64,1024]{3,2,1,0:T(8,128)}, f32[8,64,1024]{2,1,0:T(8,128)S(1)}) fusion(f32[4,8,64,1024]{3,2,1,0:T(8,128)} %get-tuple-element.387, s32[]{:T(128)} %get-tuple-element.386, bf16[8,64,1536]{1,2,0:T(8,128)(2,1)S(1)} %bitcast.165, pred[8,1536,1024]{2,1,0:T(32,128)(4,1)} %bitcast_compare_fusion.4), kind=kOutput, calls=%fused_computation.12.clone.1 | convolution fusion | flops 1610612736 | bytes 18350592 | tf_op jit(solution)/shard_map/while/body/eval_jaxpr/grk,gkl->grl/dot_general | solution.py:79
  235.6 11.5 %all_to_all.35 = f32[32,32,2]{0,2,1:T(2,128)S(1)} all-to-all(f32[32,32,2]{0,2,1:T(2,128)S(1)} %get-tuple-element.256), channel_id=1, replica_groups=mesh['corpus'=32,'query'=4] {'corpus'}, dimensions={1} | all-to-all | bytes 16384 | tf_op jit(solution)/shard_map/all_to_all | solution.py:188
  301.3 212.7 %while.28 = (s32[]{:T(128)}, f32[4,8,64,768]{3,1,0,2:T(8,128)}, f32[4,16,96,8]{1,3,2,0:T(8,128)}, s32[4,8,64,9]{2,1,3,0:T(8,128)S(1)}, f32[4,8,64,1024]{3,2,1,0:...) while((s32[]{:T(128)}, f32[4,8,64,768]{3,1,0,2:T(8,128)}, ...), condition=%wide.region_15.16_spmd.clone, body=%wide.region_13.15_spmd.clone.sunk | while | flops 1788871168 | bytes 67385192 | solution.py:129
  313.6 9.3 %bitcast_compare_fusion.5 = pred[8,1536,1024]{2,1,0:T(32,128)(4,1)} fusion(s32[1536]{0:T(1024)S(1)} %eq.184, s32[8,96,1024]{2,1,0:T(8,128)S(1)} %dynamic-slice_bitcast_fusion.15), kind=kLoop, calls=%fused_computation.19.clone.1 | loop fusion | flops 12582912 | bytes 15734784 | tf_op jit(solution)/shard_map/while/body/eval_jaxpr/eq | solution.py:54
  322.9 12.8 %fusion.84 = f32[8,64,1536]{1,2,0:T(8,128)} fusion(pred[8,1536,1024]{2,1,0:T(32,128)(4,1)} %bitcast_compare_fusion.5, f32[8,64,1024]{2,1,0:T(8,128)} %select_reduce_fusion.2, f32[4,8,64,1024]{3,2,1,0:T(8,128)} %get-tuple-element.430, s32[]{:T(128)} %get-tuple-element.415, f32[8,64]{1,0:T(8,128)S(1)} %get-tuple-element.375, ...), kind=kOutput, calls=%fused_computation.38.clone.1 | convolution fusion | flops 1613234176 | bytes 19928576 | tf_op jit(solution)/shard_map/while/body/eval_jaxpr/grl,gkl->grk/dot_general | solution.py:118
  366.7 9.3 %bitcast_compare_fusion.5 = pred[8,1536,1024]{2,1,0:T(32,128)(4,1)} fusion(s32[1536]{0:T(1024)S(1)} %eq.184, s32[8,96,1024]{2,1,0:T(8,128)S(1)} %dynamic-slice_bitcast_fusion.15), kind=kLoop, calls=%fused_computation.19.clone.1 | loop fusion | flops 12582912 | bytes 15734784 | tf_op jit(solution)/shard_map/while/body/eval_jaxpr/eq | solution.py:54
  376.0 12.8 %fusion.84 = f32[8,64,1536]{1,2,0:T(8,128)} fusion(pred[8,1536,1024]{2,1,0:T(32,128)(4,1)} %bitcast_compare_fusion.5, f32[8,64,1024]{2,1,0:T(8,128)} %select_reduce_fusion.2, f32[4,8,64,1024]{3,2,1,0:T(8,128)} %get-tuple-element.430, s32[]{:T(128)} %get-tuple-element.415, f32[8,64]{1,0:T(8,128)S(1)} %get-tuple-element.375, ...), kind=kOutput, calls=%fused_computation.38.clone.1 | convolution fusion | flops 1613234176 | bytes 19928576 | tf_op jit(solution)/shard_map/while/body/eval_jaxpr/grl,gkl->grk/dot_general | solution.py:118
  419.8 9.3 %bitcast_compare_fusion.5 = pred[8,1536,1024]{2,1,0:T(32,128)(4,1)} fusion(s32[1536]{0:T(1024)S(1)} %eq.184, s32[8,96,1024]{2,1,0:T(8,128)S(1)} %dynamic-slice_bitcast_fusion.15), kind=kLoop, calls=%fused_computation.19.clone.1 | loop fusion | flops 12582912 | bytes 15734784 | tf_op jit(solution)/shard_map/while/body/eval_jaxpr/eq | solution.py:54
  429.1 12.8 %fusion.84 = f32[8,64,1536]{1,2,0:T(8,128)} fusion(pred[8,1536,1024]{2,1,0:T(32,128)(4,1)} %bitcast_compare_fusion.5, f32[8,64,1024]{2,1,0:T(8,128)} %select_reduce_fusion.2, f32[4,8,64,1024]{3,2,1,0:T(8,128)} %get-tuple-element.430, s32[]{:T(128)} %get-tuple-element.415, f32[8,64]{1,0:T(8,128)S(1)} %get-tuple-element.375, ...), kind=kOutput, calls=%fused_computation.38.clone.1 | convolution fusion | flops 1613234176 | bytes 19928576 | tf_op jit(solution)/shard_map/while/body/eval_jaxpr/grl,gkl->grk/dot_general | solution.py:118
  472.8 9.3 %bitcast_compare_fusion.5 = pred[8,1536,1024]{2,1,0:T(32,128)(4,1)} fusion(s32[1536]{0:T(1024)S(1)} %eq.184, s32[8,96,1024]{2,1,0:T(8,128)S(1)} %dynamic-slice_bitcast_fusion.15), kind=kLoop, calls=%fused_computation.19.clone.1 | loop fusion | flops 12582912 | bytes 15734784 | tf_op jit(solution)/shard_map/while/body/eval_jaxpr/eq | solution.py:54
  482.2 12.8 %fusion.84 = f32[8,64,1536]{1,2,0:T(8,128)} fusion(pred[8,1536,1024]{2,1,0:T(32,128)(4,1)} %bitcast_compare_fusion.5, f32[8,64,1024]{2,1,0:T(8,128)} %select_reduce_fusion.2, f32[4,8,64,1024]{3,2,1,0:T(8,128)} %get-tuple-element.430, s32[]{:T(128)} %get-tuple-element.415, f32[8,64]{1,0:T(8,128)S(1)} %get-tuple-element.375, ...), kind=kOutput, calls=%fused_computation.38.clone.1 | convolution fusion | flops 1613234176 | bytes 19928576 | tf_op jit(solution)/shard_map/while/body/eval_jaxpr/grl,gkl->grk/dot_general | solution.py:118
  519.2 141.8 %psum.7 = f32[16,768]{0,1:T(8,128)S(1)} all-reduce(f32[16,768]{0,1:T(8,128)S(1)} %bitcast.174), channel_id=1, replica_groups=mesh['corpus'=32,'query'=4] {'corpus','query'}, use_global_device_ids=true, to_apply=%region_18.19 | all-reduce | flops 12288 | bytes 98304 | tf_op jit(solution)/shard_map/psum | solution.py:241
  663.2 10.3 %copy.154 = f32[32,32,2,768]{3,2,1,0:T(2,128)} copy(f32[32,32,2,768]{3,0,2,1:T(8,128)} %all-to-all-done.6) | data formatting | bytes 12582912 | tf_op jit(solution)/shard_map/all_to_all | solution.py:232
  682.1 8.7 %gather_fusion.2 = f32[1024,768]{1,0:T(8,128)} fusion(f32[2048,768]{1,0:T(8,128)} %reshape.321, s32[1024]{0:T(1024)S(1)} %copy-done.14), kind=kCustom, calls=%fused_computation.2 | custom fusion | bytes 6295552 | tf_op jit(solution)/shard_map/gather | solution.py:239
  (265 shorter events, 307.6 us)
Async XLA Ops:
  10.2 16.1 %copy-start.7 = (bf16[256,768]{1,0:T(8,128)(2,1)S(1)}, bf16[256,768]{1,0:T(8,128)(2,1)}, u32[]{:S(2)}) copy-start(bf16[256,768]{1,0:T(8,128)(2,1)} %param.9) | copy-start | bytes 1179652
  10.9 17.1 %copy-start.15 = (s32[1024,1]{0,1:T(1,128)}, s32[1024,1]{0,1:T(1,128)S(1)}, u32[]{:S(2)}) copy-start(s32[1024,1]{0,1:T(1,128)S(1)} %compare_select_fusion.1) | copy-start | bytes 12292
  16.7 28.0 %all-to-all-start = ((s32[32,1,576]{2,1,0:T(1,128)}), s32[32,1,576]{2,1,0:T(1,128)S(1)}, u32[]{:S(2)}, u32[]{:S(2)}) async-start(s32[32,1,576]{2,1,0:T(1,128)} %reshape.393), calls=%async_computation | async-start | bytes 163840 | tf_op jit(solution)/shard_map/all_to_all | solution.py:173
  44.7 47.1 %all-to-all-start.1 = ((bf16[32,32,2,768]{3,2,0,1:T(2,128)(2,1)}), bf16[32,32,2,768]{3,2,0,1:T(2,128)(2,1)S(1)}, u32[]{:S(2)}, u32[]{:S(2)}) async-start(bf16[32,32,2,768]{3,2,0,1:T(2,128)(2,1)} %copy.136), calls=%async_computation.1 | async-start | bytes 6291456 | tf_op jit(solution)/shard_map/all_to_all | solution.py:166
  112.8 9.4 %copy-start = (bf16[8,64,96,16]{1,3,2,0:T(8,128)(2,1)S(1)}, bf16[8,64,96,16]{1,3,2,0:T(8,128)(2,1)}, u32[]{:S(2)}) copy-start(bf16[8,64,96,16]{1,3,2,0:T(8,128)(2,1)} %copy.181) | copy-start | bytes 4718596 | tf_op jit(solution)/shard_map/while
  145.2 9.4 %copy-start = (bf16[8,64,96,16]{1,3,2,0:T(8,128)(2,1)S(1)}, bf16[8,64,96,16]{1,3,2,0:T(8,128)(2,1)}, u32[]{:S(2)}) copy-start(bf16[8,64,96,16]{1,3,2,0:T(8,128)(2,1)} %copy.181) | copy-start | bytes 4718596 | tf_op jit(solution)/shard_map/while
  177.6 9.4 %copy-start = (bf16[8,64,96,16]{1,3,2,0:T(8,128)(2,1)S(1)}, bf16[8,64,96,16]{1,3,2,0:T(8,128)(2,1)}, u32[]{:S(2)}) copy-start(bf16[8,64,96,16]{1,3,2,0:T(8,128)(2,1)} %copy.181) | copy-start | bytes 4718596 | tf_op jit(solution)/shard_map/while
  210.0 9.4 %copy-start = (bf16[8,64,96,16]{1,3,2,0:T(8,128)(2,1)S(1)}, bf16[8,64,96,16]{1,3,2,0:T(8,128)(2,1)}, u32[]{:S(2)}) copy-start(bf16[8,64,96,16]{1,3,2,0:T(8,128)(2,1)} %copy.181) | copy-start | bytes 4718596 | tf_op jit(solution)/shard_map/while
  247.1 12.3 %all-to-all-start.4 = ((f32[32,32,2]{0,2,1:T(2,128)}), f32[32,32,2]{0,2,1:T(2,128)S(1)}, u32[]{:S(2)}, u32[]{:S(2)}) async-start(f32[32,32,2]{0,2,1:T(2,128)} %get-tuple-element.255), calls=%async_computation.4 | async-start | bytes 65536 | tf_op jit(solution)/shard_map/all_to_all | solution.py:195
  252.2 14.2 %copy-start.13 = (s32[1024]{0:T(1024)}, s32[1024]{0:T(1024)S(1)}, u32[]{:S(2)}) copy-start(s32[1024]{0:T(1024)S(1)} %broadcast_clamp_fusion) | copy-start | bytes 12292
  259.4 34.5 %copy-start.4 = (s32[32,32,2,9]{0,2,1,3:T(2,128)S(1)}, s32[32,32,2,9]{0,2,1,3:T(2,128)}, u32[]{:S(2)}) copy-start(s32[32,32,2,9]{0,2,1,3:T(2,128)} %copy-done.3) | copy-start | bytes 221188
  272.8 14.8 %all-to-all-start.5 = ((f32[32,32,2]{0,2,1:T(2,128)}), f32[32,32,2]{0,2,1:T(2,128)S(1)}, u32[]{:S(2)}, u32[]{:S(2)}) async-start(f32[32,32,2]{0,2,1:T(2,128)} %copy.148), calls=%async_computation.5 | async-start | bytes 65536 | tf_op jit(solution)/shard_map/all_to_all | solution.py:217
  287.6 13.5 %all-to-all-start.3 = ((f32[32,32,2]{0,2,1:T(2,128)}), f32[32,32,2]{0,2,1:T(2,128)S(1)}, u32[]{:S(2)}, u32[]{:S(2)}) async-start(f32[32,32,2]{0,2,1:T(2,128)} %copy.144), calls=%async_computation.3 | async-start | bytes 65536 | tf_op jit(solution)/shard_map/all_to_all | solution.py:210
  301.5 8.5 %copy-start.5 = (s32[4,8,64,9]{2,1,3,0:T(8,128)}, s32[4,8,64,9]{2,1,3,0:T(8,128)S(1)}, u32[]{:S(2)}) copy-start(s32[4,8,64,9]{2,1,3,0:T(8,128)S(1)} %get-tuple-element.429) | copy-start | bytes 221188 | tf_op jit(solution)/shard_map/while
  346.3 8.3 %copy-start.6 = (s32[4,8,64,9]{2,1,3,0:T(8,128)S(1)}, s32[4,8,64,9]{2,1,3,0:T(8,128)}, u32[]{:S(2)}) copy-start(s32[4,8,64,9]{2,1,3,0:T(8,128)} %copy-done.5) | copy-start | bytes 221188 | tf_op jit(solution)/shard_map/while
  346.3 8.3 %copy-start.10 = (f32[4,8,64]{2,1,0:T(8,128)S(1)}, f32[4,8,64]{2,1,0:T(8,128)}, u32[]{:S(2)}) copy-start(f32[4,8,64]{2,1,0:T(8,128)} %copy-done.9) | copy-start | bytes 24580 | tf_op jit(solution)/shard_map/while
  346.3 8.3 %copy-start.12 = (f32[4,8,64]{2,1,0:T(8,128)S(1)}, f32[4,8,64]{2,1,0:T(8,128)}, u32[]{:S(2)}) copy-start(f32[4,8,64]{2,1,0:T(8,128)} %copy-done.11) | copy-start | bytes 24580 | tf_op jit(solution)/shard_map/while
  354.6 8.5 %copy-start.5 = (s32[4,8,64,9]{2,1,3,0:T(8,128)}, s32[4,8,64,9]{2,1,3,0:T(8,128)S(1)}, u32[]{:S(2)}) copy-start(s32[4,8,64,9]{2,1,3,0:T(8,128)S(1)} %get-tuple-element.429) | copy-start | bytes 221188 | tf_op jit(solution)/shard_map/while
  407.7 8.5 %copy-start.5 = (s32[4,8,64,9]{2,1,3,0:T(8,128)}, s32[4,8,64,9]{2,1,3,0:T(8,128)S(1)}, u32[]{:S(2)}) copy-start(s32[4,8,64,9]{2,1,3,0:T(8,128)S(1)} %get-tuple-element.429) | copy-start | bytes 221188 | tf_op jit(solution)/shard_map/while
  452.5 8.3 %copy-start.10 = (f32[4,8,64]{2,1,0:T(8,128)S(1)}, f32[4,8,64]{2,1,0:T(8,128)}, u32[]{:S(2)}) copy-start(f32[4,8,64]{2,1,0:T(8,128)} %copy-done.9) | copy-start | bytes 24580 | tf_op jit(solution)/shard_map/while
  452.5 8.3 %copy-start.12 = (f32[4,8,64]{2,1,0:T(8,128)S(1)}, f32[4,8,64]{2,1,0:T(8,128)}, u32[]{:S(2)}) copy-start(f32[4,8,64]{2,1,0:T(8,128)} %copy-done.11) | copy-start | bytes 24580 | tf_op jit(solution)/shard_map/while
  460.8 8.5 %copy-start.5 = (s32[4,8,64,9]{2,1,3,0:T(8,128)}, s32[4,8,64,9]{2,1,3,0:T(8,128)S(1)}, u32[]{:S(2)}) copy-start(s32[4,8,64,9]{2,1,3,0:T(8,128)S(1)} %get-tuple-element.429) | copy-start | bytes 221188 | tf_op jit(solution)/shard_map/while
  514.1 149.2 %all-to-all-start.6 = ((f32[32,32,2,768]{3,0,2,1:T(8,128)}), f32[32,32,2,768]{3,0,2,1:T(8,128)}, u32[]{:S(2)}, u32[]{:S(2)}) async-start(f32[32,32,2,768]{3,0,2,1:T(8,128)} %bitcast.170), calls=%async_computation.6 | async-start | bytes 12582912 | tf_op jit(solution)/shard_map/all_to_all | solution.py:232
  673.5 8.5 %copy-start.14 = (s32[1024]{0:T(1024)S(1)}, s32[1024]{0:T(1024)}, u32[]{:S(2)}) copy-start(s32[1024]{0:T(1024)} %copy-done.13) | copy-start | bytes 12292
  (20 other events, 78.3 us)
where the time goes:
time: 708 us; the launch traced here: 697 us
  matrix products  170 us (24%)
  local copies, waits for them, and re-layouts  168 us (24%)
  blocking collectives  153 us (22%)
  other arithmetic  125 us (18%)
  starting transfers between devices  40.1 us (6%)
  waiting for transfers between devices  38.7 us (5%)
    psum x1, blocking collectives, shards(): book_sum = lax.psum(book_part, ('corpus', 'query'))  142 us
    eq x8, other arithmetic, code_one_hot(): marked = code_block[:, :, None, :] == levels[None, None, :, None]  74.8 us
    dot_general x4, matrix products, grad_piece(): jnp.einsum('grl,gkl->grk', grad_scores, one_hot, preferred_element_type=j...  51.3 us
    dot_general x4, matrix products, score_piece(): jnp.einsum('grk,gkl->grl', lut_rows, one_hot, preferred_element_type=jnp....  46.8 us
    dot_general x4, matrix products, grad_piece(): jnp.einsum('grmk,grme->kme', histogram, split_rows, precision=highest)  33 us
    all_to_all x1, waiting for transfers between devices, shards(): lax.all_to_all(sending.reshape(lists_dev, corpus_size, capacity, D), 'cor...  31.6 us
    eq x24, local copies, waits for them, and re-layouts, code_one_hot(): marked = code_block[:, :, None, :] == levels[None, None, :, None]  28.9 us
    reduce_sum x4, other arithmetic, grad_piece(): jnp.sum(jnp.where(target_spot[:, :, :, None] == places, weights[:, None],...  28.5 us
  transfers between devices with their start and end apart: 6, of which 3 were waited for; matrix products, arithmetic and copies ran while one was open for 6% of the time, Pallas kernels for 0%

commit v1 on v0

--- a/solution.py
+++ b/solution.py
@@ -238,7 +238,7 @@
     )
     per_probe = returned.reshape(slot_count, D)[placed].reshape(query_rows, PROBES, D)
     grad_queries = jnp.sum(per_probe, axis=1)
-    book_sum = lax.psum(book_part, ("corpus", "query"))
+    book_sum = lax.psum(lax.psum(book_part, "query"), "corpus")
     normed = book_sum * lax.rsqrt(jnp.mean(book_sum * book_sum) + EPSILON)
     return (grad_queries.astype(jnp.bfloat16), normed)
 

time: 708 us -> 759 us (1.072)
  blocking collectives: 153 us -> 200 us
    psum x1 -> x2, blocking collectives: 142 us -> 189 us  [shards(): book_sum = lax.psum(lax.psum(book_part, 'query'), 'corpus')]
where the time goes in v1:
time: 759 us; the launch traced here: 744 us
  blocking collectives  200 us (26%)
  matrix products  170 us (22%)
  local copies, waits for them, and re-layouts  168 us (22%)
  other arithmetic  125 us (16%)
  starting transfers between devices  40.1 us (5%)
  waiting for transfers between devices  38.7 us (5%)
    psum x2, blocking collectives, shards(): book_sum = lax.psum(lax.psum(book_part, 'query'), 'corpus')  189 us
    eq x8, other arithmetic, code_one_hot(): marked = code_block[:, :, None, :] == levels[None, None, :, None]  74.8 us
    dot_general x4, matrix products, grad_piece(): jnp.einsum('grl,gkl->grk', grad_scores, one_hot, preferred_element_type=j...  51.3 us
    dot_general x4, matrix products, score_piece(): jnp.einsum('grk,gkl->grl', lut_rows, one_hot, preferred_element_type=jnp....  46.8 us
    dot_general x4, matrix products, grad_piece(): jnp.einsum('grmk,grme->kme', histogram, split_rows, precision=highest)  33 us
    all_to_all x1, waiting for transfers between devices, shards(): lax.all_to_all(sending.reshape(lists_dev, corpus_size, capacity, D), 'cor...  31.6 us
    eq x24, local copies, waits for them, and re-layouts, code_one_hot(): marked = code_block[:, :, None, :] == levels[None, None, :, None]  28.9 us
    reduce_sum x4, other arithmetic, grad_piece(): jnp.sum(jnp.where(target_spot[:, :, :, None] == places, weights[:, None],...  28.5 us
  transfers between devices with their start and end apart: 6, of which 3 were waited for; matrix products, arithmetic and copies ran while one was open for 6% of the time, Pallas kernels for 0%

profile of v1, /device:TPU:1, one launch (start us, length us, event | category | flops | bytes accessed | tf_op | source)
XLA Modules:
  0.0 743.9 jit_solution(16586258859005661835)
XLA Ops:
  16.7 9.6 %all-to-all-start = ((s32[32,1,576]{2,1,0:T(1,128)}), s32[32,1,576]{2,1,0:T(1,128)S(1)}, u32[]{:S(2)}, u32[]{:S(2)}) async-start(s32[32,1,576]{2,1,0:T(1,128)} %reshape.393), calls=%async_computation | async-start | bytes 163840 | tf_op jit(solution)/shard_map/all_to_all | solution.py:173
  60.2 31.6 %all-to-all-done.1 = bf16[32,32,2,768]{3,2,0,1:T(2,128)(2,1)S(1)} async-done(((bf16[32,32,2,768]{3,2,0,1:T(2,128)(2,1)}), bf16[32,32,2,768]{3,2,0,1:T(2,128)(2,1)S(1)}, u32[]{:S(2)}, u32[]{:S(2)}) %all-to-all-start.1) | async-done | bytes 3145760 | tf_op jit(solution)/shard_map/all_to_all | solution.py:166
  102.7 129.6 %while.27 = (s32[]{:T(128)}, f32[4,8,64,1024]{3,2,1,0:T(8,128)}, f32[4,8,64]{2,1,0:T(8,128)}, f32[4,8,64]{2,1,0:T(8,128)}, bf16[4,8,64,768]{2,3,1,0:T(8,128)(2,1...) while((s32[]{:T(128)}, f32[4,8,64,1024]{3,2,1,0:T(8,128)}, ...), condition=%wide.region_8.9_spmd, body=%wide.region_5.8_spmd.sunk | while | flops 1701051392 | bytes 57241216 | solution.py:84
  112.8 9.4 %bitcast_compare_fusion.4 = pred[8,1536,1024]{2,1,0:T(32,128)(4,1)} fusion(s32[1536]{0:T(1024)S(1)} %eq.177, s32[8,96,1024]{2,1,0:T(8,128)S(1)} %dynamic-slice_bitcast_fusion.14), kind=kLoop, calls=%fused_computation.9.clone.1 | loop fusion | flops 12582912 | bytes 15734784 | tf_op jit(solution)/shard_map/while/body/eval_jaxpr/eq | solution.py:54
  122.1 11.7 %bitcast_dynamic-update-slice_fusion.5 = (f32[4,8,64,1024]{3,2,1,0:T(8,128)}, f32[8,64,1024]{2,1,0:T(8,128)S(1)}) fusion(f32[4,8,64,1024]{3,2,1,0:T(8,128)} %get-tuple-element.387, s32[]{:T(128)} %get-tuple-element.386, bf16[8,64,1536]{1,2,0:T(8,128)(2,1)S(1)} %bitcast.165, pred[8,1536,1024]{2,1,0:T(32,128)(4,1)} %bitcast_compare_fusion.4), kind=kOutput, calls=%fused_computation.12.clone.1 | convolution fusion | flops 1610612736 | bytes 18350592 | tf_op jit(solution)/shard_map/while/body/eval_jaxpr/grk,gkl->grl/dot_general | solution.py:79
  145.2 9.4 %bitcast_compare_fusion.4 = pred[8,1536,1024]{2,1,0:T(32,128)(4,1)} fusion(s32[1536]{0:T(1024)S(1)} %eq.177, s32[8,96,1024]{2,1,0:T(8,128)S(1)} %dynamic-slice_bitcast_fusion.14), kind=kLoop, calls=%fused_computation.9.clone.1 | loop fusion | flops 12582912 | bytes 15734784 | tf_op jit(solution)/shard_map/while/body/eval_jaxpr/eq | solution.py:54
  154.5 11.7 %bitcast_dynamic-update-slice_fusion.5 = (f32[4,8,64,1024]{3,2,1,0:T(8,128)}, f32[8,64,1024]{2,1,0:T(8,128)S(1)}) fusion(f32[4,8,64,1024]{3,2,1,0:T(8,128)} %get-tuple-element.387, s32[]{:T(128)} %get-tuple-element.386, bf16[8,64,1536]{1,2,0:T(8,128)(2,1)S(1)} %bitcast.165, pred[8,1536,1024]{2,1,0:T(32,128)(4,1)} %bitcast_compare_fusion.4), kind=kOutput, calls=%fused_computation.12.clone.1 | convolution fusion | flops 1610612736 | bytes 18350592 | tf_op jit(solution)/shard_map/while/body/eval_jaxpr/grk,gkl->grl/dot_general | solution.py:79
  177.6 9.4 %bitcast_compare_fusion.4 = pred[8,1536,1024]{2,1,0:T(32,128)(4,1)} fusion(s32[1536]{0:T(1024)S(1)} %eq.177, s32[8,96,1024]{2,1,0:T(8,128)S(1)} %dynamic-slice_bitcast_fusion.14), kind=kLoop, calls=%fused_computation.9.clone.1 | loop fusion | flops 12582912 | bytes 15734784 | tf_op jit(solution)/shard_map/while/body/eval_jaxpr/eq | solution.py:54
  186.9 11.7 %bitcast_dynamic-update-slice_fusion.5 = (f32[4,8,64,1024]{3,2,1,0:T(8,128)}, f32[8,64,1024]{2,1,0:T(8,128)S(1)}) fusion(f32[4,8,64,1024]{3,2,1,0:T(8,128)} %get-tuple-element.387, s32[]{:T(128)} %get-tuple-element.386, bf16[8,64,1536]{1,2,0:T(8,128)(2,1)S(1)} %bitcast.165, pred[8,1536,1024]{2,1,0:T(32,128)(4,1)} %bitcast_compare_fusion.4), kind=kOutput, calls=%fused_computation.12.clone.1 | convolution fusion | flops 1610612736 | bytes 18350592 | tf_op jit(solution)/shard_map/while/body/eval_jaxpr/grk,gkl->grl/dot_general | solution.py:79
  210.0 9.4 %bitcast_compare_fusion.4 = pred[8,1536,1024]{2,1,0:T(32,128)(4,1)} fusion(s32[1536]{0:T(1024)S(1)} %eq.177, s32[8,96,1024]{2,1,0:T(8,128)S(1)} %dynamic-slice_bitcast_fusion.14), kind=kLoop, calls=%fused_computation.9.clone.1 | loop fusion | flops 12582912 | bytes 15734784 | tf_op jit(solution)/shard_map/while/body/eval_jaxpr/eq | solution.py:54
  219.4 11.7 %bitcast_dynamic-update-slice_fusion.5 = (f32[4,8,64,1024]{3,2,1,0:T(8,128)}, f32[8,64,1024]{2,1,0:T(8,128)S(1)}) fusion(f32[4,8,64,1024]{3,2,1,0:T(8,128)} %get-tuple-element.387, s32[]{:T(128)} %get-tuple-element.386, bf16[8,64,1536]{1,2,0:T(8,128)(2,1)S(1)} %bitcast.165, pred[8,1536,1024]{2,1,0:T(32,128)(4,1)} %bitcast_compare_fusion.4), kind=kOutput, calls=%fused_computation.12.clone.1 | convolution fusion | flops 1610612736 | bytes 18350592 | tf_op jit(solution)/shard_map/while/body/eval_jaxpr/grk,gkl->grl/dot_general | solution.py:79
  235.6 11.5 %all_to_all.35 = f32[32,32,2]{0,2,1:T(2,128)S(1)} all-to-all(f32[32,32,2]{0,2,1:T(2,128)S(1)} %get-tuple-element.256), channel_id=1, replica_groups=mesh['corpus'=32,'query'=4] {'corpus'}, dimensions={1} | all-to-all | bytes 16384 | tf_op jit(solution)/shard_map/all_to_all | solution.py:188
  301.3 212.7 %while.28 = (s32[]{:T(128)}, f32[4,8,64,768]{3,1,0,2:T(8,128)}, f32[4,16,96,8]{1,3,2,0:T(8,128)}, s32[4,8,64,9]{2,1,3,0:T(8,128)S(1)}, f32[4,8,64,1024]{3,2,1,0:...) while((s32[]{:T(128)}, f32[4,8,64,768]{3,1,0,2:T(8,128)}, ...), condition=%wide.region_15.16_spmd.clone, body=%wide.region_13.15_spmd.clone.sunk | while | flops 1788871168 | bytes 67385192 | solution.py:129
  313.6 9.3 %bitcast_compare_fusion.5 = pred[8,1536,1024]{2,1,0:T(32,128)(4,1)} fusion(s32[1536]{0:T(1024)S(1)} %eq.184, s32[8,96,1024]{2,1,0:T(8,128)S(1)} %dynamic-slice_bitcast_fusion.15), kind=kLoop, calls=%fused_computation.19.clone.1 | loop fusion | flops 12582912 | bytes 15734784 | tf_op jit(solution)/shard_map/while/body/eval_jaxpr/eq | solution.py:54
  322.9 12.8 %fusion.84 = f32[8,64,1536]{1,2,0:T(8,128)} fusion(pred[8,1536,1024]{2,1,0:T(32,128)(4,1)} %bitcast_compare_fusion.5, f32[8,64,1024]{2,1,0:T(8,128)} %select_reduce_fusion.2, f32[4,8,64,1024]{3,2,1,0:T(8,128)} %get-tuple-element.430, s32[]{:T(128)} %get-tuple-element.415, f32[8,64]{1,0:T(8,128)S(1)} %get-tuple-element.375, ...), kind=kOutput, calls=%fused_computation.38.clone.1 | convolution fusion | flops 1613234176 | bytes 19928576 | tf_op jit(solution)/shard_map/while/body/eval_jaxpr/grl,gkl->grk/dot_general | solution.py:118
  366.7 9.3 %bitcast_compare_fusion.5 = pred[8,1536,1024]{2,1,0:T(32,128)(4,1)} fusion(s32[1536]{0:T(1024)S(1)} %eq.184, s32[8,96,1024]{2,1,0:T(8,128)S(1)} %dynamic-slice_bitcast_fusion.15), kind=kLoop, calls=%fused_computation.19.clone.1 | loop fusion | flops 12582912 | bytes 15734784 | tf_op jit(solution)/shard_map/while/body/eval_jaxpr/eq | solution.py:54
  376.0 12.8 %fusion.84 = f32[8,64,1536]{1,2,0:T(8,128)} fusion(pred[8,1536,1024]{2,1,0:T(32,128)(4,1)} %bitcast_compare_fusion.5, f32[8,64,1024]{2,1,0:T(8,128)} %select_reduce_fusion.2, f32[4,8,64,1024]{3,2,1,0:T(8,128)} %get-tuple-element.430, s32[]{:T(128)} %get-tuple-element.415, f32[8,64]{1,0:T(8,128)S(1)} %get-tuple-element.375, ...), kind=kOutput, calls=%fused_computation.38.clone.1 | convolution fusion | flops 1613234176 | bytes 19928576 | tf_op jit(solution)/shard_map/while/body/eval_jaxpr/grl,gkl->grk/dot_general | solution.py:118
  419.8 9.3 %bitcast_compare_fusion.5 = pred[8,1536,1024]{2,1,0:T(32,128)(4,1)} fusion(s32[1536]{0:T(1024)S(1)} %eq.184, s32[8,96,1024]{2,1,0:T(8,128)S(1)} %dynamic-slice_bitcast_fusion.15), kind=kLoop, calls=%fused_computation.19.clone.1 | loop fusion | flops 12582912 | bytes 15734784 | tf_op jit(solution)/shard_map/while/body/eval_jaxpr/eq | solution.py:54
  429.1 12.8 %fusion.84 = f32[8,64,1536]{1,2,0:T(8,128)} fusion(pred[8,1536,1024]{2,1,0:T(32,128)(4,1)} %bitcast_compare_fusion.5, f32[8,64,1024]{2,1,0:T(8,128)} %select_reduce_fusion.2, f32[4,8,64,1024]{3,2,1,0:T(8,128)} %get-tuple-element.430, s32[]{:T(128)} %get-tuple-element.415, f32[8,64]{1,0:T(8,128)S(1)} %get-tuple-element.375, ...), kind=kOutput, calls=%fused_computation.38.clone.1 | convolution fusion | flops 1613234176 | bytes 19928576 | tf_op jit(solution)/shard_map/while/body/eval_jaxpr/grl,gkl->grk/dot_general | solution.py:118
  472.8 9.3 %bitcast_compare_fusion.5 = pred[8,1536,1024]{2,1,0:T(32,128)(4,1)} fusion(s32[1536]{0:T(1024)S(1)} %eq.184, s32[8,96,1024]{2,1,0:T(8,128)S(1)} %dynamic-slice_bitcast_fusion.15), kind=kLoop, calls=%fused_computation.19.clone.1 | loop fusion | flops 12582912 | bytes 15734784 | tf_op jit(solution)/shard_map/while/body/eval_jaxpr/eq | solution.py:54
  482.2 12.8 %fusion.84 = f32[8,64,1536]{1,2,0:T(8,128)} fusion(pred[8,1536,1024]{2,1,0:T(32,128)(4,1)} %bitcast_compare_fusion.5, f32[8,64,1024]{2,1,0:T(8,128)} %select_reduce_fusion.2, f32[4,8,64,1024]{3,2,1,0:T(8,128)} %get-tuple-element.430, s32[]{:T(128)} %get-tuple-element.415, f32[8,64]{1,0:T(8,128)S(1)} %get-tuple-element.375, ...), kind=kOutput, calls=%fused_computation.38.clone.1 | convolution fusion | flops 1613234176 | bytes 19928576 | tf_op jit(solution)/shard_map/while/body/eval_jaxpr/grl,gkl->grk/dot_general | solution.py:118
  519.2 18.1 %psum.14 = f32[16,768]{0,1:T(8,128)S(1)} all-reduce(f32[16,768]{0,1:T(8,128)S(1)} %bitcast.174), channel_id=1, replica_groups=mesh['corpus'=32,'query'=4] {'query'}, use_global_device_ids=true, to_apply=%region_18.19 | all-reduce | flops 12288 | bytes 98304 | tf_op jit(solution)/shard_map/psum | solution.py:241
  537.3 170.5 %psum.15 = f32[16,768]{0,1:T(8,128)S(1)} all-reduce(f32[16,768]{0,1:T(8,128)S(1)} %psum.14), channel_id=1, replica_groups=mesh['corpus'=32,'query'=4] {'corpus'}, use_global_device_ids=true, to_apply=%region_19.20 | all-reduce | flops 12288 | bytes 98304 | tf_op jit(solution)/shard_map/psum | solution.py:241
  710.0 10.3 %copy.154 = f32[32,32,2,768]{3,2,1,0:T(2,128)} copy(f32[32,32,2,768]{3,0,2,1:T(8,128)} %all-to-all-done.6) | data formatting | bytes 12582912 | tf_op jit(solution)/shard_map/all_to_all | solution.py:232
  (266 shorter events, 316.3 us)
Async XLA Ops:
  10.2 16.1 %copy-start.7 = (bf16[256,768]{1,0:T(8,128)(2,1)S(1)}, bf16[256,768]{1,0:T(8,128)(2,1)}, u32[]{:S(2)}) copy-start(bf16[256,768]{1,0:T(8,128)(2,1)} %param.9) | copy-start | bytes 1179652
  10.9 17.1 %copy-start.15 = (s32[1024,1]{0,1:T(1,128)}, s32[1024,1]{0,1:T(1,128)S(1)}, u32[]{:S(2)}) copy-start(s32[1024,1]{0,1:T(1,128)S(1)} %compare_select_fusion.1) | copy-start | bytes 12292
  16.7 28.0 %all-to-all-start = ((s32[32,1,576]{2,1,0:T(1,128)}), s32[32,1,576]{2,1,0:T(1,128)S(1)}, u32[]{:S(2)}, u32[]{:S(2)}) async-start(s32[32,1,576]{2,1,0:T(1,128)} %reshape.393), calls=%async_computation | async-start | bytes 163840 | tf_op jit(solution)/shard_map/all_to_all | solution.py:173
  44.7 47.1 %all-to-all-start.1 = ((bf16[32,32,2,768]{3,2,0,1:T(2,128)(2,1)}), bf16[32,32,2,768]{3,2,0,1:T(2,128)(2,1)S(1)}, u32[]{:S(2)}, u32[]{:S(2)}) async-start(bf16[32,32,2,768]{3,2,0,1:T(2,128)(2,1)} %copy.136), calls=%async_computation.1 | async-start | bytes 6291456 | tf_op jit(solution)/shard_map/all_to_all | solution.py:166
  112.8 9.4 %copy-start = (bf16[8,64,96,16]{1,3,2,0:T(8,128)(2,1)S(1)}, bf16[8,64,96,16]{1,3,2,0:T(8,128)(2,1)}, u32[]{:S(2)}) copy-start(bf16[8,64,96,16]{1,3,2,0:T(8,128)(2,1)} %copy.181) | copy-start | bytes 4718596 | tf_op jit(solution)/shard_map/while
  145.2 9.4 %copy-start = (bf16[8,64,96,16]{1,3,2,0:T(8,128)(2,1)S(1)}, bf16[8,64,96,16]{1,3,2,0:T(8,128)(2,1)}, u32[]{:S(2)}) copy-start(bf16[8,64,96,16]{1,3,2,0:T(8,128)(2,1)} %copy.181) | copy-start | bytes 4718596 | tf_op jit(solution)/shard_map/while
  177.6 9.4 %copy-start = (bf16[8,64,96,16]{1,3,2,0:T(8,128)(2,1)S(1)}, bf16[8,64,96,16]{1,3,2,0:T(8,128)(2,1)}, u32[]{:S(2)}) copy-start(bf16[8,64,96,16]{1,3,2,0:T(8,128)(2,1)} %copy.181) | copy-start | bytes 4718596 | tf_op jit(solution)/shard_map/while
  210.0 9.4 %copy-start = (bf16[8,64,96,16]{1,3,2,0:T(8,128)(2,1)S(1)}, bf16[8,64,96,16]{1,3,2,0:T(8,128)(2,1)}, u32[]{:S(2)}) copy-start(bf16[8,64,96,16]{1,3,2,0:T(8,128)(2,1)} %copy.181) | copy-start | bytes 4718596 | tf_op jit(solution)/shard_map/while
  247.1 12.3 %all-to-all-start.4 = ((f32[32,32,2]{0,2,1:T(2,128)}), f32[32,32,2]{0,2,1:T(2,128)S(1)}, u32[]{:S(2)}, u32[]{:S(2)}) async-start(f32[32,32,2]{0,2,1:T(2,128)} %get-tuple-element.255), calls=%async_computation.4 | async-start | bytes 65536 | tf_op jit(solution)/shard_map/all_to_all | solution.py:195
  252.2 14.2 %copy-start.13 = (s32[1024]{0:T(1024)}, s32[1024]{0:T(1024)S(1)}, u32[]{:S(2)}) copy-start(s32[1024]{0:T(1024)S(1)} %broadcast_clamp_fusion) | copy-start | bytes 12292
  259.4 34.5 %copy-start.4 = (s32[32,32,2,9]{0,2,1,3:T(2,128)S(1)}, s32[32,32,2,9]{0,2,1,3:T(2,128)}, u32[]{:S(2)}) copy-start(s32[32,32,2,9]{0,2,1,3:T(2,128)} %copy-done.3) | copy-start | bytes 221188
  272.8 14.8 %all-to-all-start.5 = ((f32[32,32,2]{0,2,1:T(2,128)}), f32[32,32,2]{0,2,1:T(2,128)S(1)}, u32[]{:S(2)}, u32[]{:S(2)}) async-start(f32[32,32,2]{0,2,1:T(2,128)} %copy.148), calls=%async_computation.5 | async-start | bytes 65536 | tf_op jit(solution)/shard_map/all_to_all | solution.py:217
  287.6 13.5 %all-to-all-start.3 = ((f32[32,32,2]{0,2,1:T(2,128)}), f32[32,32,2]{0,2,1:T(2,128)S(1)}, u32[]{:S(2)}, u32[]{:S(2)}) async-start(f32[32,32,2]{0,2,1:T(2,128)} %copy.144), calls=%async_computation.3 | async-start | bytes 65536 | tf_op jit(solution)/shard_map/all_to_all | solution.py:210
  301.5 8.5 %copy-start.5 = (s32[4,8,64,9]{2,1,3,0:T(8,128)}, s32[4,8,64,9]{2,1,3,0:T(8,128)S(1)}, u32[]{:S(2)}) copy-start(s32[4,8,64,9]{2,1,3,0:T(8,128)S(1)} %get-tuple-element.429) | copy-start | bytes 221188 | tf_op jit(solution)/shard_map/while
  346.3 8.3 %copy-start.6 = (s32[4,8,64,9]{2,1,3,0:T(8,128)S(1)}, s32[4,8,64,9]{2,1,3,0:T(8,128)}, u32[]{:S(2)}) copy-start(s32[4,8,64,9]{2,1,3,0:T(8,128)} %copy-done.5) | copy-start | bytes 221188 | tf_op jit(solution)/shard_map/while
  346.3 8.3 %copy-start.10 = (f32[4,8,64]{2,1,0:T(8,128)S(1)}, f32[4,8,64]{2,1,0:T(8,128)}, u32[]{:S(2)}) copy-start(f32[4,8,64]{2,1,0:T(8,128)} %copy-done.9) | copy-start | bytes 24580 | tf_op jit(solution)/shard_map/while
  346.3 8.3 %copy-start.12 = (f32[4,8,64]{2,1,0:T(8,128)S(1)}, f32[4,8,64]{2,1,0:T(8,128)}, u32[]{:S(2)}) copy-start(f32[4,8,64]{2,1,0:T(8,128)} %copy-done.11) | copy-start | bytes 24580 | tf_op jit(solution)/shard_map/while
  354.6 8.5 %copy-start.5 = (s32[4,8,64,9]{2,1,3,0:T(8,128)}, s32[4,8,64,9]{2,1,3,0:T(8,128)S(1)}, u32[]{:S(2)}) copy-start(s32[4,8,64,9]{2,1,3,0:T(8,128)S(1)} %get-tuple-element.429) | copy-start | bytes 221188 | tf_op jit(solution)/shard_map/while
  407.7 8.5 %copy-start.5 = (s32[4,8,64,9]{2,1,3,0:T(8,128)}, s32[4,8,64,9]{2,1,3,0:T(8,128)S(1)}, u32[]{:S(2)}) copy-start(s32[4,8,64,9]{2,1,3,0:T(8,128)S(1)} %get-tuple-element.429) | copy-start | bytes 221188 | tf_op jit(solution)/shard_map/while
  452.5 8.3 %copy-start.10 = (f32[4,8,64]{2,1,0:T(8,128)S(1)}, f32[4,8,64]{2,1,0:T(8,128)}, u32[]{:S(2)}) copy-start(f32[4,8,64]{2,1,0:T(8,128)} %copy-done.9) | copy-start | bytes 24580 | tf_op jit(solution)/shard_map/while
  452.5 8.3 %copy-start.12 = (f32[4,8,64]{2,1,0:T(8,128)S(1)}, f32[4,8,64]{2,1,0:T(8,128)}, u32[]{:S(2)}) copy-start(f32[4,8,64]{2,1,0:T(8,128)} %copy-done.11) | copy-start | bytes 24580 | tf_op jit(solution)/shard_map/while
  460.8 8.5 %copy-start.5 = (s32[4,8,64,9]{2,1,3,0:T(8,128)}, s32[4,8,64,9]{2,1,3,0:T(8,128)S(1)}, u32[]{:S(2)}) copy-start(s32[4,8,64,9]{2,1,3,0:T(8,128)S(1)} %get-tuple-element.429) | copy-start | bytes 221188 | tf_op jit(solution)/shard_map/while
  514.1 195.9 %all-to-all-start.6 = ((f32[32,32,2,768]{3,0,2,1:T(8,128)}), f32[32,32,2,768]{3,0,2,1:T(8,128)}, u32[]{:S(2)}, u32[]{:S(2)}) async-start(f32[32,32,2,768]{3,0,2,1:T(8,128)} %bitcast.170), calls=%async_computation.6 | async-start | bytes 12582912 | tf_op jit(solution)/shard_map/all_to_all | solution.py:232
  720.3 8.5 %copy-start.14 = (s32[1024]{0:T(1024)S(1)}, s32[1024]{0:T(1024)}, u32[]{:S(2)}) copy-start(s32[1024]{0:T(1024)} %copy-done.13) | copy-start | bytes 12292
  (20 other events, 78.3 us)
